TPU v7x, 32 devices: a whole 2x2x4 slice. The times are simulated.
32 devices in a mesh: grp: 2 (over y), frame: 4 (over x, core), band: 4 (over z).
Axes of the slice: x: 2, y: 2, z: 4, core: 2. Of those that a mesh axis runs over, the one named last changes fastest.
Arguments:
- features: bfloat16 [16, 64, 128, 256], P(('grp', 'frame'), 'band'), parts along dimension 0, may hold values from -6 to 6
- space_kernel: bfloat16 [3, 3, 256, 256], replicated, may hold values from -0.125 to 0.125
- space_gain: float32 [256], replicated, may hold values from 0.5 to 2
- space_bias: float32 [256], replicated, may hold values from -3 to 3
- time_kernel: bfloat16 [3, 256, 256], replicated, may hold values from -0.21875 to 0.21875
- time_gain: float32 [256], replicated, may hold values from 0.5 to 2
- time_bias: float32 [256], replicated, may hold values from -3 to 3
Outputs:
- decoded: bfloat16 [16, 64, 128, 256], P(('grp', 'frame'), 'band'), parts along dimension 0
There are 2 independent parts, one for each index of `grp`. A program takes and returns all parts, laid end to end along the dimension named above; an argument that names none is the same for every part. Nothing has to cross between parts.
All inputs are finite; a program needn't handle non-finite values.
Results may differ from a plain program's by a relative error of at most 0.0056.
Values may be sent and summed in bfloat16 or wider, within the bound.
A program may use at most 64 MiB of HBM per device.

v0:
```python
import functools

import jax
import jax.numpy as jnp
from jax import lax
from jax.experimental import pallas as pl
from jax.experimental.pallas import tpu as pltpu
from jax.sharding import PartitionSpec as P

LAGS = 2


def rms_silu(values, gain):
    mean = jnp.mean(values * values, axis=-1, keepdims=True)
    half = values * lax.rsqrt(mean + 1e-06) * (0.5 * gain)
    return half + half * jnp.tanh(half)


def dot(left, right):
    return jnp.dot(left, right, preferred_element_type=jnp.float32)


def kernel(
    features, space_kernel, space_gain, space_bias, time_kernel, time_gain, time_bias,
    out,
    feat, normed, hidden, ntime, earlier, wspace, wtime, vectors,
    feat_sem, weight_sem, halo_send, halo_recv, time_send, time_recv,
):
    frames, rows, cols, channels = features.shape
    half = cols // 2
    last = rows - 1
    band, bands = lax.axis_index("band"), lax.axis_size("band")
    frame, frame_parts = lax.axis_index("frame"), lax.axis_size("frame")
    has_up, has_down = band > 0, band < bands - 1
    has_prev, has_next = frame > 0, frame < frame_parts - 1
    neighbours = (
        (has_up, {"band": band - 1}),
        (has_down, {"band": band + 1}),
        (has_prev, {"frame": frame - 1}),
        (has_next, {"frame": frame + 1}),
    )

    barrier = pltpu.get_barrier_semaphore()
    for present, device in neighbours:
        @pl.when(present)
        def _():
            pl.semaphore_signal(
                barrier, inc=1, device_id=device, device_id_type=pl.DeviceIdType.MESH
            )

    def row_copy(row):
        return pltpu.make_async_copy(
            features.at[:, row], feat.at[row + 1], feat_sem.at[row]
        )

    weights = [(space_kernel, wspace), (time_kernel, wtime)] + [
        (vector, vectors.at[i])
        for i, vector in enumerate((space_gain, space_bias, time_gain, time_bias))
    ]
    weight_copies = [
        pltpu.make_async_copy(source, target, weight_sem.at[i])
        for i, (source, target) in enumerate(weights)
    ]
    for i in (2, 3, 4, 5):
        weight_copies[i].start()
    for row in range(3):
        row_copy(row).start()
    weight_copies[0].start()

    def time_copy(row, sem, start=0, count=LAGS, left=0, width=cols):
        return pltpu.make_async_remote_copy(
            ntime.at[row, pl.ds(frames - LAGS + start, count), pl.ds(left, width)],
            earlier.at[row, pl.ds(start, count), pl.ds(left, width)],
            time_send.at[sem],
            time_recv.at[sem],
            device_id={"frame": frame + 1},
            device_id_type=pl.DeviceIdType.MESH,
        )

    last_copies = [
        time_copy(last, rows + side, 0, LAGS, side * half, half)
        for side in range(2)
    ]

    def vector(i):
        return vectors[i].reshape(1, channels)

    def norm_part(slot, start=0, count=frames, left=0, width=cols):
        base = max(0, min(left - 16, cols - width - 16)) if width < cols else 0
        window = min(cols, width + 16)
        size = count * window
        values = feat[slot, start : start + count, base : base + window]
        result = rms_silu(values.reshape(size, channels).astype(jnp.float32), vector(0))
        column = base + lax.rem(
            lax.broadcasted_iota(jnp.int32, (size, channels), 0), window
        )
        before = jnp.where(column == 0, 0.0, pltpu.roll(result, 1, 0))
        after = jnp.where(column == cols - 1, 0.0, pltpu.roll(result, size - 1, 0))
        for i, piece in enumerate((before, result, after)):
            kept = piece.astype(jnp.bfloat16).reshape(count, window, channels)
            normed[
                slot, start : start + count, left : left + width,
                i * channels : (i + 1) * channels,
            ] = kept[:, left - base : left - base + width]

    def space_part(row, start=0, count=frames, left=0, width=cols):
        where = (slice(start, start + count), slice(left, left + width))
        size = count * width
        total = None
        for i in range(3):
            product = dot(
                normed[(row + i, *where)].reshape(size, 3 * channels),
                wspace[i].reshape(3 * channels, channels),
            )
            total = product if total is None else total + product
        centre = feat[(row + 1, *where)].reshape(size, channels).astype(jnp.float32)
        kept = (centre + total + vector(1)).astype(jnp.bfloat16)
        shape = (count, width, channels)
        hidden[(row, *where)] = kept.reshape(shape)
        ntime[(row, *where)] = (
            rms_silu(kept.astype(jnp.float32), vector(2)).astype(jnp.bfloat16).reshape(shape)
        )

    def space_row(row):
        space_part(row)
        pl.when(has_next)(time_copy(row, row).start)

    def time_part(row, copies, left=0, width=cols):
        columns = slice(left, left + width)
        own = ntime[row, :, columns]
        totals = [
            dot(own.reshape(-1, channels), wtime[0]).reshape(own.shape)[f]
            for f in range(frames)
        ]
        for lag in range(1, min(LAGS, frames - 1) + 1):
            term = dot(own[: frames - lag].reshape(-1, channels), wtime[lag])
            for f in range(lag, frames):
                totals[f] += term[(f - lag) * width : (f - lag + 1) * width]

        @pl.when(has_prev)
        def _():
            for copy in copies:
                copy.wait_recv()

        for lag in range(1, LAGS + 1):
            count = min(lag, frames)
            past = earlier[row, LAGS - lag : LAGS - lag + count, columns]
            term = dot(past.reshape(-1, channels), wtime[lag])
            for f in range(count):
                totals[f] += term[f * width : (f + 1) * width]
        for f in range(frames):
            temporal = totals[f].astype(jnp.bfloat16).astype(jnp.float32)
            kept = hidden[row, f, columns].astype(jnp.float32)
            out[f, row, columns] = (kept + temporal + vector(3)).astype(jnp.bfloat16)

    @pl.when(jnp.logical_not(has_prev))
    def _():
        earlier[...] = jnp.zeros_like(earlier)

    @pl.when(jnp.logical_not(has_up))
    def _():
        feat[0] = jnp.zeros(feat.shape[1:], feat.dtype)

    @pl.when(jnp.logical_not(has_down))
    def _():
        feat[rows + 1] = jnp.zeros(feat.shape[1:], feat.dtype)

    for i in (2, 3, 4, 5):
        weight_copies[i].wait()
    for row in range(3):
        row_copy(row).wait()
        norm_part(row + 1)

    peers = (
        (band + bands - 1) // bands
        + 1 - (band + 1) // bands
        + (frame + frame_parts - 1) // frame_parts
        + 1 - (frame + 1) // frame_parts
    )
    pl.semaphore_wait(barrier, peers)

    to_up = pltpu.make_async_remote_copy(
        features.at[:, 0], feat.at[rows + 1], halo_send.at[0], halo_recv.at[0],
        device_id={"band": band - 1}, device_id_type=pl.DeviceIdType.MESH,
    )
    to_down = pltpu.make_async_remote_copy(
        features.at[:, rows - 1], feat.at[0], halo_send.at[1], halo_recv.at[1],
        device_id={"band": band + 1}, device_id_type=pl.DeviceIdType.MESH,
    )
    pl.when(has_up)(to_up.start)
    pl.when(has_down)(to_down.start)

    for row in range(3, rows):
        row_copy(row).start()
    weight_copies[1].start()
    weight_copies[0].wait()
    space_row(1)

    @pl.loop(2, last)
    def _(row):
        row_copy(row + 1).wait()
        norm_part(row + 2)
        space_row(row)

    pl.when(has_up)(to_down.wait_recv)
    pl.when(has_down)(to_up.wait_recv)
    norm_part(0)
    space_row(0)
    norm_part(rows + 1)
    space_part(last)

    @pl.when(has_next)
    def _():
        for copy in last_copies:
            copy.start()

    weight_copies[1].wait()
    @pl.loop(1, last)
    def _(row):
        time_part(row, [time_copy(row, row)])

    time_part(0, [time_copy(0, 0)])
    time_part(last, last_copies)

    pl.when(has_up)(to_up.wait_send)
    pl.when(has_down)(to_down.wait_send)

    @pl.when(has_next)
    def _():
        for copy in (time_copy(0, 0), *last_copies):
            copy.wait_send()

        @pl.loop(1, last)
        def _(row):
            time_copy(row, row).wait_send()


def body(features, *rest):
    frames, rows, cols, channels = features.shape
    bf16 = jnp.bfloat16
    return pl.pallas_call(
        kernel,
        out_shape=jax.ShapeDtypeStruct(features.shape, bf16),
        in_specs=[pl.BlockSpec(memory_space=pltpu.HBM)] * 7,
        out_specs=pl.BlockSpec(memory_space=pltpu.VMEM),
        scratch_shapes=[
            pltpu.VMEM((rows + 2, frames, cols, channels), bf16),
            pltpu.VMEM((rows + 2, frames, cols, 3 * channels), bf16),
            pltpu.VMEM((rows, frames, cols, channels), bf16),
            pltpu.VMEM((rows, frames, cols, channels), bf16),
            pltpu.VMEM((rows, LAGS, cols, channels), bf16),
            pltpu.VMEM(rest[0].shape, bf16),
            pltpu.VMEM(rest[3].shape, bf16),
            pltpu.VMEM((4, channels), jnp.float32),
            pltpu.SemaphoreType.DMA((rows,)),
            pltpu.SemaphoreType.DMA((6,)),
            pltpu.SemaphoreType.DMA((2,)),
            pltpu.SemaphoreType.DMA((2,)),
            pltpu.SemaphoreType.DMA((rows + 2,)),
            pltpu.SemaphoreType.DMA((rows + 2,)),
        ],
        compiler_params=pltpu.CompilerParams(
            collective_id=0, has_side_effects=True, vmem_limit_bytes=36 * 1024 * 1024
        ),
    )(*[pltpu.with_memory_space_constraint(x, pltpu.HBM) for x in (features, *rest)])


def solution(mesh):
    return jax.shard_map(
        body,
        mesh=mesh,
        in_specs=(P(("grp", "frame"), "band", None, None), P(), P(), P(), P(), P(), P()),
        out_specs=P(("grp", "frame"), "band", None, None),
        check_vma=False,
    )
```

profile of v0, /device:TPU:1, one launch (start us, length us, event | category | flops | bytes accessed | tf_op | source)
XLA Modules:
  0.0 28.1 jit_solution(7094834509739576972)
XLA Ops:
  0.0 26.8 %shard_map.73 = bf16[2,16,128,256]{3,2,1,0:T(8,128)(2,1)S(1)} custom-call(bf16[2,16,128,256]{3,2,1,0:T(8,128)(2,1)} %features.1, bf16[3,3,256,256]{3,2,1,0:T(8,128)(2,1)} %space_kernel.1, f32[256]{0:T(256)} %space_gain.1, f32[256]{0:T(256)} %space_bias.1, bf16[3,256,256]{2,1,0:T(8,128)(2,1)} %time_kernel.1, f32[256]{0:T(256)} %time_gain.1, f32[256]{0:T(256)} %time_bias.1), custom_call_target="tpu_custom_call" | custom-call | tf_op jit(solution)/shard_map/pallas_call | solution.py:241
  26.8 1.3 %copy.9 = bf16[2,16,128,256]{3,2,1,0:T(8,128)(2,1)} copy(bf16[2,16,128,256]{3,2,1,0:T(8,128)(2,1)S(1)} %shard_map.73) | data formatting | bytes 4194304
where the time goes:
time: 28.4 us; the launch traced here: 28.1 us
  Pallas kernels  26.8 us (94%)
  local copies, waits for them, and re-layouts  1.32 us (5%)
    pallas_call x1, Pallas kernels, body(): pl.pallas_call(kernel, out_shape=jax.ShapeDtypeStruct(features.shape, bf1...  26.8 us
    unnamed x1, local copies, waits for them, and re-layouts  1.32 us

commit v1 on v0

--- a/solution.py
+++ b/solution.py
@@ -20,10 +20,14 @@
     return jnp.dot(left, right, preferred_element_type=jnp.float32)
 
 
+def group_starts(last):
+    return sorted({min(max(1, start), last - 1) for start in (1, last - 5, last - 1)})
+
+
 def kernel(
     features, space_kernel, space_gain, space_bias, time_kernel, time_gain, time_bias,
     out,
-    feat, normed, hidden, ntime, earlier, wspace, wtime, vectors,
+    feat, normed, hidden, ntime, earlier, partial, wspace, wtime, vectors,
     feat_sem, weight_sem, halo_send, halo_recv, time_send, time_recv,
 ):
     frames, rows, cols, channels = features.shape
@@ -48,39 +52,48 @@
                 barrier, inc=1, device_id=device, device_id_type=pl.DeviceIdType.MESH
             )
 
-    def row_copy(row):
+    def row_copy(row, sem):
         return pltpu.make_async_copy(
-            features.at[:, row], feat.at[row + 1], feat_sem.at[row]
-        )
-
-    weights = [(space_kernel, wspace), (time_kernel, wtime)] + [
-        (vector, vectors.at[i])
+            features.at[:, row], feat.at[row + 1], feat_sem.at[sem]
+        )
+
+    def rows_wait(start, count, sem):
+        block = feat.at[pl.ds(start + 1, count)]
+        pltpu.make_async_copy(block, block, feat_sem.at[sem]).wait()
+
+    vector_copies = [
+        pltpu.make_async_copy(vector, vectors.at[i], weight_sem.at[0])
         for i, vector in enumerate((space_gain, space_bias, time_gain, time_bias))
     ]
-    weight_copies = [
-        pltpu.make_async_copy(source, target, weight_sem.at[i])
-        for i, (source, target) in enumerate(weights)
-    ]
-    for i in (2, 3, 4, 5):
-        weight_copies[i].start()
+    vectors_copy = pltpu.make_async_copy(vectors, vectors, weight_sem.at[0])
+    space_copy = pltpu.make_async_copy(space_kernel, wspace, weight_sem.at[1])
+    lags_copy = pltpu.make_async_copy(time_kernel, wtime, weight_sem.at[2])
     for row in range(3):
-        row_copy(row).start()
-    weight_copies[0].start()
-
-    def time_copy(row, sem, start=0, count=LAGS, left=0, width=cols):
+        row_copy(row, 0).start()
+    for copy in vector_copies:
+        copy.start()
+    space_copy.start()
+
+    groups = group_starts(last)
+
+    def time_copy(source, row, sem, left=0, width=cols):
         return pltpu.make_async_remote_copy(
-            ntime.at[row, pl.ds(frames - LAGS + start, count), pl.ds(left, width)],
-            earlier.at[row, pl.ds(start, count), pl.ds(left, width)],
-            time_send.at[sem],
+            source.at[:, pl.ds(left, width)],
+            earlier.at[row, :, pl.ds(left, width)],
+            time_send.at[0],
             time_recv.at[sem],
             device_id={"frame": frame + 1},
             device_id_type=pl.DeviceIdType.MESH,
         )
 
-    last_copies = [
-        time_copy(last, rows + side, 0, LAGS, side * half, half)
-        for side in range(2)
-    ]
+    def row_send(row, sem, left=0, width=cols):
+        source = ntime.at[row, pl.ds(frames - LAGS, LAGS)]
+        pl.when(has_next)(time_copy(source, row, sem, left, width).start)
+
+    def time_wait(block, sem):
+        pl.when(has_prev)(
+            pltpu.make_async_copy(block, block, time_recv.at[sem]).wait
+        )
 
     def vector(i):
         return vectors[i].reshape(1, channels)
@@ -121,13 +134,8 @@
             rms_silu(kept.astype(jnp.float32), vector(2)).astype(jnp.bfloat16).reshape(shape)
         )
 
-    def space_row(row):
-        space_part(row)
-        pl.when(has_next)(time_copy(row, row).start)
-
-    def time_part(row, copies, left=0, width=cols):
-        columns = slice(left, left + width)
-        own = ntime[row, :, columns]
+    def own_totals(row):
+        own = ntime[row]
         totals = [
             dot(own.reshape(-1, channels), wtime[0]).reshape(own.shape)[f]
             for f in range(frames)
@@ -135,23 +143,32 @@
         for lag in range(1, min(LAGS, frames - 1) + 1):
             term = dot(own[: frames - lag].reshape(-1, channels), wtime[lag])
             for f in range(lag, frames):
-                totals[f] += term[(f - lag) * width : (f - lag + 1) * width]
-
-        @pl.when(has_prev)
-        def _():
-            for copy in copies:
-                copy.wait_recv()
-
+                totals[f] += term[(f - lag) * cols : (f - lag + 1) * cols]
+        return totals
+
+    def finish(row, f, total, left=0, width=cols):
+        columns = slice(left, left + width)
+        temporal = total.astype(jnp.bfloat16).astype(jnp.float32)
+        kept = hidden[row, f, columns].astype(jnp.float32)
+        out[f, row, columns] = (kept + temporal + vector(3)).astype(jnp.bfloat16)
+
+    def time_part(row):
+        totals = own_totals(row)
         for lag in range(1, LAGS + 1):
-            count = min(lag, frames)
-            past = earlier[row, LAGS - lag : LAGS - lag + count, columns]
+            past = earlier[row, LAGS - lag :]
             term = dot(past.reshape(-1, channels), wtime[lag])
-            for f in range(count):
-                totals[f] += term[f * width : (f + 1) * width]
+            for f in range(lag):
+                totals[f] += term[f * cols : (f + 1) * cols]
         for f in range(frames):
-            temporal = totals[f].astype(jnp.bfloat16).astype(jnp.float32)
-            kept = hidden[row, f, columns].astype(jnp.float32)
-            out[f, row, columns] = (kept + temporal + vector(3)).astype(jnp.bfloat16)
+            finish(row, f, totals[f])
+
+    def lag_sums(row):
+        for f in range(LAGS):
+            total = None
+            for lag in range(f + 1, LAGS + 1):
+                term = dot(ntime[row, frames - lag + f], wtime[lag])
+                total = term if total is None else total + term
+            partial[f] = total.astype(jnp.bfloat16)
 
     @pl.when(jnp.logical_not(has_prev))
     def _():
@@ -165,11 +182,15 @@
     def _():
         feat[rows + 1] = jnp.zeros(feat.shape[1:], feat.dtype)
 
-    for i in (2, 3, 4, 5):
-        weight_copies[i].wait()
-    for row in range(3):
-        row_copy(row).wait()
-        norm_part(row + 1)
+    vectors_copy.wait()
+    rows_wait(0, 3, 0)
+    for slot in (1, 2, 3):
+        norm_part(slot, 0, frames, 0, half)
+    space_copy.wait()
+    for row in range(3, rows):
+        row_copy(row, 1 if row == 3 else 2).start()
+    lags_copy.start()
+    space_part(1, 0, frames, 0, half)
 
     peers = (
         (band + bands - 1) // bands
@@ -190,49 +211,69 @@
     pl.when(has_up)(to_up.start)
     pl.when(has_down)(to_down.start)
 
-    for row in range(3, rows):
-        row_copy(row).start()
-    weight_copies[1].start()
-    weight_copies[0].wait()
-    space_row(1)
-
-    @pl.loop(2, last)
+    row_send(1, 0, 0, half)
+    for slot in (1, 2, 3):
+        norm_part(slot, 0, frames, half, cols - half)
+    space_part(1, 0, frames, half, cols - half)
+    row_send(1, 0, half, cols - half)
+    rows_wait(3, 1, 1)
+    norm_part(4)
+    space_part(2)
+    row_send(2, 0)
+    rows_wait(4, rows - 4, 2)
+
+    @pl.loop(3, last)
     def _(row):
-        row_copy(row + 1).wait()
         norm_part(row + 2)
-        space_row(row)
+        space_part(row)
+        row_send(row, sum((row >= g).astype(jnp.int32) for g in groups[1:]))
 
     pl.when(has_up)(to_down.wait_recv)
     pl.when(has_down)(to_up.wait_recv)
     norm_part(0)
-    space_row(0)
+    space_part(0)
+    row_send(0, len(groups))
     norm_part(rows + 1)
     space_part(last)
+    lags_copy.wait()
 
     @pl.when(has_next)
     def _():
-        for copy in last_copies:
-            copy.start()
-
-    weight_copies[1].wait()
+        lag_sums(last)
+        for side in range(2):
+            time_copy(
+                partial, last, len(groups) + 1 + side, side * half, half
+            ).start()
+
     @pl.loop(1, last)
     def _(row):
-        time_part(row, [time_copy(row, row)])
-
-    time_part(0, [time_copy(0, 0)])
-    time_part(last, last_copies)
+        for i, start in enumerate(groups):
+            end = groups[i + 1] if i + 1 < len(groups) else last
+
+            @pl.when(row == start)
+            def _():
+                time_wait(earlier.at[pl.ds(start, end - start)], i)
+
+        time_part(row)
+
+    time_wait(earlier.at[0], len(groups))
+    time_part(0)
+    totals = own_totals(last)
+    for side in range(2):
+        columns = slice(side * half, (side + 1) * half)
+        time_wait(earlier.at[last, :, pl.ds(side * half, half)], len(groups) + 1 + side)
+        for f in range(frames):
+            total = totals[f][columns]
+            if f < LAGS:
+                total += earlier[last, f, columns].astype(jnp.float32)
+            finish(last, f, total, side * half, half)
 
     pl.when(has_up)(to_up.wait_send)
     pl.when(has_down)(to_down.wait_send)
 
     @pl.when(has_next)
     def _():
-        for copy in (time_copy(0, 0), *last_copies):
-            copy.wait_send()
-
-        @pl.loop(1, last)
-        def _(row):
-            time_copy(row, row).wait_send()
+        pltpu.make_async_copy(earlier, earlier, time_send.at[0]).wait()
 
 
 def body(features, *rest):
@@ -249,15 +290,16 @@
             pltpu.VMEM((rows, frames, cols, channels), bf16),
             pltpu.VMEM((rows, frames, cols, channels), bf16),
             pltpu.VMEM((rows, LAGS, cols, channels), bf16),
+            pltpu.VMEM((LAGS, cols, channels), bf16),
             pltpu.VMEM(rest[0].shape, bf16),
             pltpu.VMEM(rest[3].shape, bf16),
             pltpu.VMEM((4, channels), jnp.float32),
-            pltpu.SemaphoreType.DMA((rows,)),
-            pltpu.SemaphoreType.DMA((6,)),
+            pltpu.SemaphoreType.DMA((3,)),
+            pltpu.SemaphoreType.DMA((3,)),
             pltpu.SemaphoreType.DMA((2,)),
             pltpu.SemaphoreType.DMA((2,)),
-            pltpu.SemaphoreType.DMA((rows + 2,)),
-            pltpu.SemaphoreType.DMA((rows + 2,)),
+            pltpu.SemaphoreType.DMA((1,)),
+            pltpu.SemaphoreType.DMA((len(group_starts(rows - 1)) + 3,)),
         ],
         compiler_params=pltpu.CompilerParams(
             collective_id=0, has_side_effects=True, vmem_limit_bytes=36 * 1024 * 1024

time: 28.4 us -> 27.4 us (0.965)
  Pallas kernels: 26.8 us -> 25.7 us
    pallas_call x1, Pallas kernels: 26.8 us -> 25.7 us  [body(): pl.pallas_call(kernel, out_shape=jax.ShapeDtypeStruct(features.shape, bf1...]
where the time goes in v1:
time: 27.4 us; the launch traced here: 27.1 us
  Pallas kernels  25.7 us (94%)
  local copies, waits for them, and re-layouts  1.32 us (5%)
    pallas_call x1, Pallas kernels, body(): pl.pallas_call(kernel, out_shape=jax.ShapeDtypeStruct(features.shape, bf1...  25.7 us
    unnamed x1, local copies, waits for them, and re-layouts  1.32 us

profile of v1, /device:TPU:1, one launch (start us, length us, event | category | flops | bytes accessed | tf_op | source)
XLA Modules:
  0.0 27.1 jit_solution(1234520130993990862)
XLA Ops:
  0.0 25.7 %shard_map.73 = bf16[2,16,128,256]{3,2,1,0:T(8,128)(2,1)S(1)} custom-call(bf16[2,16,128,256]{3,2,1,0:T(8,128)(2,1)} %features.1, bf16[3,3,256,256]{3,2,1,0:T(8,128)(2,1)} %space_kernel.1, f32[256]{0:T(256)} %space_gain.1, f32[256]{0:T(256)} %space_bias.1, bf16[3,256,256]{2,1,0:T(8,128)(2,1)} %time_kernel.1, f32[256]{0:T(256)} %time_gain.1, f32[256]{0:T(256)} %time_bias.1), custom_call_target="tpu_custom_call" | custom-call | tf_op jit(solution)/shard_map/pallas_call | solution.py:282
  25.7 1.3 %copy.9 = bf16[2,16,128,256]{3,2,1,0:T(8,128)(2,1)} copy(bf16[2,16,128,256]{3,2,1,0:T(8,128)(2,1)S(1)} %shard_map.73) | data formatting | bytes 4194304

commit v2 on v1

--- a/solution.py
+++ b/solution.py
@@ -32,6 +32,7 @@
 ):
     frames, rows, cols, channels = features.shape
     half = cols // 2
+    split = frames - LAGS + 1
     last = rows - 1
     band, bands = lax.axis_index("band"), lax.axis_size("band")
     frame, frame_parts = lax.axis_index("frame"), lax.axis_size("frame")
@@ -45,20 +46,26 @@
     )
 
     barrier = pltpu.get_barrier_semaphore()
-    for present, device in neighbours:
+
+    def greet(present, device):
         @pl.when(present)
         def _():
             pl.semaphore_signal(
                 barrier, inc=1, device_id=device, device_id_type=pl.DeviceIdType.MESH
             )
 
-    def row_copy(row, sem):
-        return pltpu.make_async_copy(
-            features.at[:, row], feat.at[row + 1], feat_sem.at[sem]
-        )
-
-    def rows_wait(start, count, sem):
-        block = feat.at[pl.ds(start + 1, count)]
+    def rows_start(first, count, sem, start=0, size=frames, step=None):
+        step = step or count
+        for f in range(start, start + size):
+            for row in range(first, first + count, step):
+                pltpu.make_async_copy(
+                    features.at[f, pl.ds(row, step)],
+                    feat.at[pl.ds(row + 1, step), f],
+                    feat_sem.at[sem],
+                ).start()
+
+    def rows_wait(first, count, sem, start=0, size=frames):
+        block = feat.at[pl.ds(first + 1, count), pl.ds(start, size)]
         pltpu.make_async_copy(block, block, feat_sem.at[sem]).wait()
 
     vector_copies = [
@@ -66,29 +73,38 @@
         for i, vector in enumerate((space_gain, space_bias, time_gain, time_bias))
     ]
     vectors_copy = pltpu.make_async_copy(vectors, vectors, weight_sem.at[0])
-    space_copy = pltpu.make_async_copy(space_kernel, wspace, weight_sem.at[1])
-    lags_copy = pltpu.make_async_copy(time_kernel, wtime, weight_sem.at[2])
-    for row in range(3):
-        row_copy(row, 0).start()
+    space_copies = [
+        pltpu.make_async_copy(space_kernel.at[i], wspace.at[i], weight_sem.at[1 + i])
+        for i in range(3)
+    ]
+    lags_copy = pltpu.make_async_copy(time_kernel, wtime, weight_sem.at[4])
+    rows_start(0, 3, 0, 0, split, 1)
     for copy in vector_copies:
         copy.start()
-    space_copy.start()
+    greet(*neighbours[2])
+    for copy in space_copies:
+        copy.start()
+    for i in (0, 1, 3):
+        greet(*neighbours[i])
+    rows_start(0, 4, 1, split, frames - split)
+    rows_start(3, 1, 2, 0, split)
 
     groups = group_starts(last)
 
-    def time_copy(source, row, sem, left=0, width=cols):
+    def time_copy(source, target, sem):
         return pltpu.make_async_remote_copy(
-            source.at[:, pl.ds(left, width)],
-            earlier.at[row, :, pl.ds(left, width)],
+            source,
+            target,
             time_send.at[0],
             time_recv.at[sem],
             device_id={"frame": frame + 1},
             device_id_type=pl.DeviceIdType.MESH,
         )
 
-    def row_send(row, sem, left=0, width=cols):
-        source = ntime.at[row, pl.ds(frames - LAGS, LAGS)]
-        pl.when(has_next)(time_copy(source, row, sem, left, width).start)
+    def row_send(row, sem, start=0, count=LAGS):
+        source = ntime.at[row, pl.ds(frames - LAGS + start, count)]
+        target = earlier.at[row, pl.ds(start, count)]
+        pl.when(has_next)(time_copy(source, target, sem).start)
 
     def time_wait(block, sem):
         pl.when(has_prev)(
@@ -98,41 +114,50 @@
     def vector(i):
         return vectors[i].reshape(1, channels)
 
-    def norm_part(slot, start=0, count=frames, left=0, width=cols):
-        base = max(0, min(left - 16, cols - width - 16)) if width < cols else 0
-        window = min(cols, width + 16)
-        size = count * window
-        values = feat[slot, start : start + count, base : base + window]
+    def norm_part(slot, start=0, count=frames):
+        size = count * cols
+        values = feat[slot, start : start + count]
         result = rms_silu(values.reshape(size, channels).astype(jnp.float32), vector(0))
-        column = base + lax.rem(
-            lax.broadcasted_iota(jnp.int32, (size, channels), 0), window
-        )
+        column = lax.rem(lax.broadcasted_iota(jnp.int32, (size, channels), 0), cols)
         before = jnp.where(column == 0, 0.0, pltpu.roll(result, 1, 0))
         after = jnp.where(column == cols - 1, 0.0, pltpu.roll(result, size - 1, 0))
         for i, piece in enumerate((before, result, after)):
-            kept = piece.astype(jnp.bfloat16).reshape(count, window, channels)
             normed[
-                slot, start : start + count, left : left + width,
-                i * channels : (i + 1) * channels,
-            ] = kept[:, left - base : left - base + width]
-
-    def space_part(row, start=0, count=frames, left=0, width=cols):
-        where = (slice(start, start + count), slice(left, left + width))
-        size = count * width
+                slot, start : start + count, :, i * channels : (i + 1) * channels
+            ] = piece.astype(jnp.bfloat16).reshape(count, cols, channels)
+
+    def taps(block, chosen, start, count):
         total = None
-        for i in range(3):
-            product = dot(
-                normed[(row + i, *where)].reshape(size, 3 * channels),
-                wspace[i].reshape(3 * channels, channels),
-            )
-            total = product if total is None else total + product
-        centre = feat[(row + 1, *where)].reshape(size, channels).astype(jnp.float32)
-        kept = (centre + total + vector(1)).astype(jnp.bfloat16)
-        shape = (count, width, channels)
-        hidden[(row, *where)] = kept.reshape(shape)
-        ntime[(row, *where)] = (
-            rms_silu(kept.astype(jnp.float32), vector(2)).astype(jnp.bfloat16).reshape(shape)
-        )
+        for i, low, high in chosen:
+            columns = slice(low * channels, high * channels)
+            parts = [
+                normed[row + i, start : start + count, :, columns]
+                for row in block
+            ]
+            parts = [part.reshape(-1, (high - low) * channels) for part in parts]
+            left = parts[0] if len(parts) == 1 else jnp.concatenate(parts, 0)
+            term = dot(left, wspace[i, low:high].reshape(-1, channels))
+            total = term if total is None else total + term
+        return total
+
+    def space_store(block, total, start, count):
+        size = count * cols
+        shape = (count, cols, channels)
+        where = slice(start, start + count)
+        for i, row in enumerate(block):
+            centre = feat[row + 1, where].reshape(size, channels).astype(jnp.float32)
+            summed = centre + total[i * size : (i + 1) * size] + vector(1)
+            kept = summed.astype(jnp.bfloat16)
+            hidden[row, where] = kept.reshape(shape)
+            after = rms_silu(kept.astype(jnp.float32), vector(2))
+            ntime[row, where] = after.astype(jnp.bfloat16).reshape(shape)
+
+    def space_part(block, start=0, count=frames):
+        total = taps(block, ((0, 0, 3), (1, 0, 3), (2, 0, 3)), start, count)
+        space_store(block, total, start, count)
+
+    def once(step):
+        pl.loop(0, 1 + band // bands)(lambda _: step())
 
     def own_totals(row):
         own = ntime[row]
@@ -183,14 +208,18 @@
         feat[rows + 1] = jnp.zeros(feat.shape[1:], feat.dtype)
 
     vectors_copy.wait()
-    rows_wait(0, 3, 0)
+    rows_wait(0, 3, 0, 0, split)
     for slot in (1, 2, 3):
-        norm_part(slot, 0, frames, 0, half)
-    space_copy.wait()
-    for row in range(3, rows):
-        row_copy(row, 1 if row == 3 else 2).start()
-    lags_copy.start()
-    space_part(1, 0, frames, 0, half)
+        norm_part(slot, 0, split)
+    space_copies[0].wait()
+
+    @once
+    def _():
+        total = taps((1,), ((0, 0, 3),), 0, split)
+        space_copies[1].wait()
+        total += taps((1,), ((1, 0, 3),), 0, split)
+        space_copies[2].wait()
+        space_store((1,), total + taps((1,), ((2, 0, 3),), 0, split), 0, split)
 
     peers = (
         (band + bands - 1) // bands
@@ -211,38 +240,61 @@
     pl.when(has_up)(to_up.start)
     pl.when(has_down)(to_down.start)
 
-    row_send(1, 0, 0, half)
-    for slot in (1, 2, 3):
-        norm_part(slot, 0, frames, half, cols - half)
-    space_part(1, 0, frames, half, cols - half)
-    row_send(1, 0, half, cols - half)
-    rows_wait(3, 1, 1)
-    norm_part(4)
-    space_part(2)
-    row_send(2, 0)
-    rows_wait(4, rows - 4, 2)
+    row_send(1, 0, 0, 1)
+    rows_start(4, rows - 4, 3)
+    lags_copy.start()
+    rows_wait(0, 4, 1, split, frames - split)
+    rows_wait(3, 1, 2, 0, split)
+
+    @once
+    def _():
+        for slot in (1, 2, 3, 4):
+            norm_part(slot, split, frames - split)
+        space_part((1, 2), split, frames - split)
+
+    for row in (1, 2):
+        row_send(row, 0, 1, LAGS - 1)
+
+    @once
+    def _():
+        norm_part(4, 0, split)
+        space_part((2,), 0, split)
+
+    row_send(2, 0, 0, 1)
+    rows_wait(4, rows - 4, 3)
 
     @pl.loop(3, last)
     def _(row):
         norm_part(row + 2)
-        space_part(row)
+        space_part((row,))
         row_send(row, sum((row >= g).astype(jnp.int32) for g in groups[1:]))
 
     pl.when(has_up)(to_down.wait_recv)
     pl.when(has_down)(to_up.wait_recv)
-    norm_part(0)
-    space_part(0)
+
+    @once
+    def _():
+        norm_part(0)
+        space_part((0,))
+
     row_send(0, len(groups))
-    norm_part(rows + 1)
-    space_part(last)
+
+    @once
+    def _():
+        norm_part(rows + 1)
+        space_part((last,))
+
     lags_copy.wait()
 
     @pl.when(has_next)
     def _():
         lag_sums(last)
         for side in range(2):
+            columns = pl.ds(side * half, half)
             time_copy(
-                partial, last, len(groups) + 1 + side, side * half, half
+                partial.at[:, columns],
+                earlier.at[last, :, columns],
+                len(groups) + 1 + side,
             ).start()
 
     @pl.loop(1, last)
@@ -294,8 +346,8 @@
             pltpu.VMEM(rest[0].shape, bf16),
             pltpu.VMEM(rest[3].shape, bf16),
             pltpu.VMEM((4, channels), jnp.float32),
-            pltpu.SemaphoreType.DMA((3,)),
-            pltpu.SemaphoreType.DMA((3,)),
+            pltpu.SemaphoreType.DMA((4,)),
+            pltpu.SemaphoreType.DMA((5,)),
             pltpu.SemaphoreType.DMA((2,)),
             pltpu.SemaphoreType.DMA((2,)),
             pltpu.SemaphoreType.DMA((1,)),

time: 27.4 us -> 27.4 us (level)
  no operation moved by 1% of the time
where the time goes in v2:
time: 27.4 us; the launch traced here: 27.1 us
  Pallas kernels  25.8 us (94%)
  local copies, waits for them, and re-layouts  1.32 us (5%)
    pallas_call x1, Pallas kernels, body(): pl.pallas_call(kernel, out_shape=jax.ShapeDtypeStruct(features.shape, bf1...  25.8 us
    unnamed x1, local copies, waits for them, and re-layouts  1.32 us

profile of v2, /device:TPU:1, one launch (start us, length us, event | category | flops | bytes accessed | tf_op | source)
XLA Modules:
  0.0 27.1 jit_solution(7308536074976892502)
XLA Ops:
  0.0 25.8 %shard_map.73 = bf16[2,16,128,256]{3,2,1,0:T(8,128)(2,1)S(1)} custom-call(bf16[2,16,128,256]{3,2,1,0:T(8,128)(2,1)} %features.1, bf16[3,3,256,256]{3,2,1,0:T(8,128)(2,1)} %space_kernel.1, f32[256]{0:T(256)} %space_gain.1, f32[256]{0:T(256)} %space_bias.1, bf16[3,256,256]{2,1,0:T(8,128)(2,1)} %time_kernel.1, f32[256]{0:T(256)} %time_gain.1, f32[256]{0:T(256)} %time_bias.1), custom_call_target="tpu_custom_call" | custom-call | tf_op jit(solution)/shard_map/pallas_call | solution.py:334
  25.8 1.3 %copy.9 = bf16[2,16,128,256]{3,2,1,0:T(8,128)(2,1)} copy(bf16[2,16,128,256]{3,2,1,0:T(8,128)(2,1)S(1)} %shard_map.73) | data formatting | bytes 4194304

commit v3 on v2

--- a/solution.py
+++ b/solution.py
@@ -74,10 +74,14 @@
     ]
     vectors_copy = pltpu.make_async_copy(vectors, vectors, weight_sem.at[0])
     space_copies = [
-        pltpu.make_async_copy(space_kernel.at[i], wspace.at[i], weight_sem.at[1 + i])
-        for i in range(3)
+        pltpu.make_async_copy(
+            space_kernel.at[pl.ds(start, count)],
+            wspace.at[pl.ds(start, count)],
+            weight_sem.at[sem],
+        )
+        for start, count, sem in ((0, 2, 1), (2, 1, 2))
     ]
-    lags_copy = pltpu.make_async_copy(time_kernel, wtime, weight_sem.at[4])
+    lags_copy = pltpu.make_async_copy(time_kernel, wtime, weight_sem.at[3])
     rows_start(0, 3, 0, 0, split, 1)
     for copy in vector_copies:
         copy.start()
@@ -140,21 +144,21 @@
             total = term if total is None else total + term
         return total
 
-    def space_store(block, total, start, count):
-        size = count * cols
+    def space_store(row, total, start, count):
         shape = (count, cols, channels)
         where = slice(start, start + count)
+        centre = feat[row + 1, where].reshape(-1, channels).astype(jnp.float32)
+        kept = (centre + total + vector(1)).astype(jnp.bfloat16)
+        hidden[row, where] = kept.reshape(shape)
+        after = rms_silu(kept.astype(jnp.float32), vector(2))
+        ntime[row, where] = after.astype(jnp.bfloat16).reshape(shape)
+
+    def space_part(block, start=0, count=frames, stored=lambda row: None):
+        total = taps(block, ((0, 0, 3), (1, 0, 3), (2, 0, 3)), start, count)
+        size = count * cols
         for i, row in enumerate(block):
-            centre = feat[row + 1, where].reshape(size, channels).astype(jnp.float32)
-            summed = centre + total[i * size : (i + 1) * size] + vector(1)
-            kept = summed.astype(jnp.bfloat16)
-            hidden[row, where] = kept.reshape(shape)
-            after = rms_silu(kept.astype(jnp.float32), vector(2))
-            ntime[row, where] = after.astype(jnp.bfloat16).reshape(shape)
-
-    def space_part(block, start=0, count=frames):
-        total = taps(block, ((0, 0, 3), (1, 0, 3), (2, 0, 3)), start, count)
-        space_store(block, total, start, count)
+            space_store(row, total[i * size : (i + 1) * size], start, count)
+            stored(row)
 
     def once(step):
         pl.loop(0, 1 + band // bands)(lambda _: step())
@@ -215,11 +219,9 @@
 
     @once
     def _():
-        total = taps((1,), ((0, 0, 3),), 0, split)
+        total = taps((1,), ((0, 0, 3), (1, 0, 3)), 0, split)
         space_copies[1].wait()
-        total += taps((1,), ((1, 0, 3),), 0, split)
-        space_copies[2].wait()
-        space_store((1,), total + taps((1,), ((2, 0, 3),), 0, split), 0, split)
+        space_store(1, total + taps((1,), ((2, 0, 3),), 0, split), 0, split)
 
     peers = (
         (band + bands - 1) // bands
@@ -229,6 +231,7 @@
     )
     pl.semaphore_wait(barrier, peers)
 
+    row_send(1, 0, 0, 1)
     to_up = pltpu.make_async_remote_copy(
         features.at[:, 0], feat.at[rows + 1], halo_send.at[0], halo_recv.at[0],
         device_id={"band": band - 1}, device_id_type=pl.DeviceIdType.MESH,
@@ -240,7 +243,6 @@
     pl.when(has_up)(to_up.start)
     pl.when(has_down)(to_down.start)
 
-    row_send(1, 0, 0, 1)
     rows_start(4, rows - 4, 3)
     lags_copy.start()
     rows_wait(0, 4, 1, split, frames - split)
@@ -250,10 +252,9 @@
     def _():
         for slot in (1, 2, 3, 4):
             norm_part(slot, split, frames - split)
-        space_part((1, 2), split, frames - split)
-
-    for row in (1, 2):
-        row_send(row, 0, 1, LAGS - 1)
+        space_part(
+            (1, 2), split, frames - split, lambda row: row_send(row, 0, 1, LAGS - 1)
+        )
 
     @once
     def _():
@@ -347,7 +348,7 @@
             pltpu.VMEM(rest[3].shape, bf16),
             pltpu.VMEM((4, channels), jnp.float32),
             pltpu.SemaphoreType.DMA((4,)),
-            pltpu.SemaphoreType.DMA((5,)),
+            pltpu.SemaphoreType.DMA((4,)),
             pltpu.SemaphoreType.DMA((2,)),
             pltpu.SemaphoreType.DMA((2,)),
             pltpu.SemaphoreType.DMA((1,)),

time: 27.4 us -> 27.4 us (level)
  no operation moved by 1% of the time
where the time goes in v3:
time: 27.4 us; the launch traced here: 27.1 us
  Pallas kernels  25.7 us (94%)
  local copies, waits for them, and re-layouts  1.32 us (5%)
    pallas_call x1, Pallas kernels, body(): pl.pallas_call(kernel, out_shape=jax.ShapeDtypeStruct(features.shape, bf1...  25.7 us
    unnamed x1, local copies, waits for them, and re-layouts  1.32 us

profile of v3, /device:TPU:1, one launch (start us, length us, event | category | flops | bytes accessed | tf_op | source)
XLA Modules:
  0.0 27.1 jit_solution(13094022974100528001)
XLA Ops:
  0.0 25.7 %shard_map.73 = bf16[2,16,128,256]{3,2,1,0:T(8,128)(2,1)S(1)} custom-call(bf16[2,16,128,256]{3,2,1,0:T(8,128)(2,1)} %features.1, bf16[3,3,256,256]{3,2,1,0:T(8,128)(2,1)} %space_kernel.1, f32[256]{0:T(256)} %space_gain.1, f32[256]{0:T(256)} %space_bias.1, bf16[3,256,256]{2,1,0:T(8,128)(2,1)} %time_kernel.1, f32[256]{0:T(256)} %time_gain.1, f32[256]{0:T(256)} %time_bias.1), custom_call_target="tpu_custom_call" | custom-call | tf_op jit(solution)/shard_map/pallas_call | solution.py:335
  25.8 1.3 %copy.9 = bf16[2,16,128,256]{3,2,1,0:T(8,128)(2,1)} copy(bf16[2,16,128,256]{3,2,1,0:T(8,128)(2,1)S(1)} %shard_map.73) | data formatting | bytes 4194304

commit v4 on v3

--- a/solution.py
+++ b/solution.py
@@ -27,8 +27,8 @@
 def kernel(
     features, space_kernel, space_gain, space_bias, time_kernel, time_gain, time_bias,
     out,
-    feat, normed, hidden, ntime, earlier, partial, wspace, wtime, vectors,
-    feat_sem, weight_sem, halo_send, halo_recv, time_send, time_recv,
+    feat, normed, begun, hidden, ntime, earlier, partial, wspace, wtime, vectors,
+    feat_sem, weight_sem, halo_recv, time_recv,
 ):
     frames, rows, cols, channels = features.shape
     half = cols // 2
@@ -81,7 +81,7 @@
         )
         for start, count, sem in ((0, 2, 1), (2, 1, 2))
     ]
-    lags_copy = pltpu.make_async_copy(time_kernel, wtime, weight_sem.at[3])
+    lags_copy = pltpu.make_async_copy(time_kernel, wtime, feat_sem.at[2])
     rows_start(0, 3, 0, 0, split, 1)
     for copy in vector_copies:
         copy.start()
@@ -93,13 +93,14 @@
     rows_start(0, 4, 1, split, frames - split)
     rows_start(3, 1, 2, 0, split)
 
+    time_send, up_send, down_send = (weight_sem.at[i] for i in range(3))
     groups = group_starts(last)
 
     def time_copy(source, target, sem):
         return pltpu.make_async_remote_copy(
             source,
             target,
-            time_send.at[0],
+            time_send,
             time_recv.at[sem],
             device_id={"frame": frame + 1},
             device_id_type=pl.DeviceIdType.MESH,
@@ -219,9 +220,13 @@
 
     @once
     def _():
-        total = taps((1,), ((0, 0, 3), (1, 0, 3)), 0, split)
-        space_copies[1].wait()
-        space_store(1, total + taps((1,), ((2, 0, 3),), 0, split), 0, split)
+        begun[...] = taps((1,), ((0, 0, 3), (1, 0, 3)), 0, split)
+
+    space_copies[1].wait()
+
+    @once
+    def _():
+        space_store(1, begun[...] + taps((1,), ((2, 0, 3),), 0, split), 0, split)
 
     peers = (
         (band + bands - 1) // bands
@@ -233,20 +238,20 @@
 
     row_send(1, 0, 0, 1)
     to_up = pltpu.make_async_remote_copy(
-        features.at[:, 0], feat.at[rows + 1], halo_send.at[0], halo_recv.at[0],
+        features.at[:, 0], feat.at[rows + 1], up_send, halo_recv.at[0],
         device_id={"band": band - 1}, device_id_type=pl.DeviceIdType.MESH,
     )
     to_down = pltpu.make_async_remote_copy(
-        features.at[:, rows - 1], feat.at[0], halo_send.at[1], halo_recv.at[1],
+        features.at[:, rows - 1], feat.at[0], down_send, halo_recv.at[1],
         device_id={"band": band + 1}, device_id_type=pl.DeviceIdType.MESH,
     )
     pl.when(has_up)(to_up.start)
     pl.when(has_down)(to_down.start)
 
-    rows_start(4, rows - 4, 3)
-    lags_copy.start()
+    rows_start(4, rows - 4, 0)
     rows_wait(0, 4, 1, split, frames - split)
     rows_wait(3, 1, 2, 0, split)
+    lags_copy.start()
 
     @once
     def _():
@@ -262,7 +267,7 @@
         space_part((2,), 0, split)
 
     row_send(2, 0, 0, 1)
-    rows_wait(4, rows - 4, 3)
+    rows_wait(4, rows - 4, 0)
 
     @pl.loop(3, last)
     def _(row):
@@ -278,7 +283,7 @@
         norm_part(0)
         space_part((0,))
 
-    row_send(0, len(groups))
+    row_send(0, len(groups) - 1)
 
     @once
     def _():
@@ -295,26 +300,25 @@
             time_copy(
                 partial.at[:, columns],
                 earlier.at[last, :, columns],
-                len(groups) + 1 + side,
+                len(groups) + side,
             ).start()
 
     @pl.loop(1, last)
     def _(row):
         for i, start in enumerate(groups):
-            end = groups[i + 1] if i + 1 < len(groups) else last
+            count = groups[i + 1] - start if i + 1 < len(groups) else rows - start
 
             @pl.when(row == start)
             def _():
-                time_wait(earlier.at[pl.ds(start, end - start)], i)
+                time_wait(earlier.at[pl.ds(rows - count, count)], i)
 
         time_part(row)
 
-    time_wait(earlier.at[0], len(groups))
     time_part(0)
     totals = own_totals(last)
     for side in range(2):
         columns = slice(side * half, (side + 1) * half)
-        time_wait(earlier.at[last, :, pl.ds(side * half, half)], len(groups) + 1 + side)
+        time_wait(earlier.at[last, :, pl.ds(side * half, half)], len(groups) + side)
         for f in range(frames):
             total = totals[f][columns]
             if f < LAGS:
@@ -326,7 +330,7 @@
 
     @pl.when(has_next)
     def _():
-        pltpu.make_async_copy(earlier, earlier, time_send.at[0]).wait()
+        pltpu.make_async_copy(earlier, earlier, time_send).wait()
 
 
 def body(features, *rest):
@@ -340,6 +344,7 @@
         scratch_shapes=[
             pltpu.VMEM((rows + 2, frames, cols, channels), bf16),
             pltpu.VMEM((rows + 2, frames, cols, 3 * channels), bf16),
+            pltpu.VMEM(((frames - LAGS + 1) * cols, channels), jnp.float32),
             pltpu.VMEM((rows, frames, cols, channels), bf16),
             pltpu.VMEM((rows, frames, cols, channels), bf16),
             pltpu.VMEM((rows, LAGS, cols, channels), bf16),
@@ -347,12 +352,10 @@
             pltpu.VMEM(rest[0].shape, bf16),
             pltpu.VMEM(rest[3].shape, bf16),
             pltpu.VMEM((4, channels), jnp.float32),
-            pltpu.SemaphoreType.DMA((4,)),
-            pltpu.SemaphoreType.DMA((4,)),
+            pltpu.SemaphoreType.DMA((3,)),
+            pltpu.SemaphoreType.DMA((3,)),
             pltpu.SemaphoreType.DMA((2,)),
-            pltpu.SemaphoreType.DMA((2,)),
-            pltpu.SemaphoreType.DMA((1,)),
-            pltpu.SemaphoreType.DMA((len(group_starts(rows - 1)) + 3,)),
+            pltpu.SemaphoreType.DMA((len(group_starts(rows - 1)) + 2,)),
         ],
         compiler_params=pltpu.CompilerParams(
             collective_id=0, has_side_effects=True, vmem_limit_bytes=36 * 1024 * 1024

time: 27.4 us -> 27.3 us (level)
  no operation moved by 1% of the time
where the time goes in v4:
time: 27.3 us; the launch traced here: 27 us
  Pallas kernels  25.7 us (94%)
  local copies, waits for them, and re-layouts  1.32 us (5%)
    pallas_call x1, Pallas kernels, body(): pl.pallas_call(kernel, out_shape=jax.ShapeDtypeStruct(features.shape, bf1...  25.7 us
    unnamed x1, local copies, waits for them, and re-layouts  1.32 us

profile of v4, /device:TPU:1, one launch (start us, length us, event | category | flops | bytes accessed | tf_op | source)
XLA Modules:
  0.0 27.0 jit_solution(5145346518105517472)
XLA Ops:
  0.0 25.7 %shard_map.73 = bf16[2,16,128,256]{3,2,1,0:T(8,128)(2,1)S(1)} custom-call(bf16[2,16,128,256]{3,2,1,0:T(8,128)(2,1)} %features.1, bf16[3,3,256,256]{3,2,1,0:T(8,128)(2,1)} %space_kernel.1, f32[256]{0:T(256)} %space_gain.1, f32[256]{0:T(256)} %space_bias.1, bf16[3,256,256]{2,1,0:T(8,128)(2,1)} %time_kernel.1, f32[256]{0:T(256)} %time_gain.1, f32[256]{0:T(256)} %time_bias.1), custom_call_target="tpu_custom_call" | custom-call | tf_op jit(solution)/shard_map/pallas_call | solution.py:339
  25.7 1.3 %copy.9 = bf16[2,16,128,256]{3,2,1,0:T(8,128)(2,1)} copy(bf16[2,16,128,256]{3,2,1,0:T(8,128)(2,1)S(1)} %shard_map.73) | data formatting | bytes 4194304

commit v5 on v4

--- a/solution.py
+++ b/solution.py
@@ -79,7 +79,7 @@
             wspace.at[pl.ds(start, count)],
             weight_sem.at[sem],
         )
-        for start, count, sem in ((0, 2, 1), (2, 1, 2))
+        for start, count, sem in ((0, 4, 1), (4, 5, 2))
     ]
     lags_copy = pltpu.make_async_copy(time_kernel, wtime, feat_sem.at[2])
     rows_start(0, 3, 0, 0, split, 1)
@@ -141,7 +141,7 @@
             ]
             parts = [part.reshape(-1, (high - low) * channels) for part in parts]
             left = parts[0] if len(parts) == 1 else jnp.concatenate(parts, 0)
-            term = dot(left, wspace[i, low:high].reshape(-1, channels))
+            term = dot(left, wspace[3 * i + low : 3 * i + high].reshape(-1, channels))
             total = term if total is None else total + term
         return total
 
@@ -220,13 +220,14 @@
 
     @once
     def _():
-        begun[...] = taps((1,), ((0, 0, 3), (1, 0, 3)), 0, split)
+        begun[...] = taps((1,), ((0, 0, 3), (1, 0, 1)), 0, split)
 
     space_copies[1].wait()
 
     @once
     def _():
-        space_store(1, begun[...] + taps((1,), ((2, 0, 3),), 0, split), 0, split)
+        rest = taps((1,), ((1, 1, 3), (2, 0, 3)), 0, split)
+        space_store(1, begun[...] + rest, 0, split)
 
     peers = (
         (band + bands - 1) // bands
@@ -336,6 +337,7 @@
 def body(features, *rest):
     frames, rows, cols, channels = features.shape
     bf16 = jnp.bfloat16
+    rest = (rest[0].reshape(-1, channels, channels), *rest[1:])
     return pl.pallas_call(
         kernel,
         out_shape=jax.ShapeDtypeStruct(features.shape, bf16),

time: 27.3 us -> 27.2 us (level)
  no operation moved by 1% of the time
where the time goes in v5:
time: 27.2 us; the launch traced here: 27 us
  Pallas kernels  25.7 us (94%)
  local copies, waits for them, and re-layouts  1.32 us (5%)
    pallas_call x1, Pallas kernels, body(): pl.pallas_call(kernel, out_shape=jax.ShapeDtypeStruct(features.shape, bf1...  25.7 us
    unnamed x1, local copies, waits for them, and re-layouts  1.32 us

profile of v5, /device:TPU:1, one launch (start us, length us, event | category | flops | bytes accessed | tf_op | source)
XLA Modules:
  0.0 27.0 jit_solution(11446436514019203827)
XLA Ops:
  0.0 25.7 %shard_map.73 = bf16[2,16,128,256]{3,2,1,0:T(8,128)(2,1)S(1)} custom-call(bf16[2,16,128,256]{3,2,1,0:T(8,128)(2,1)} %features.1, bf16[9,256,256]{2,1,0:T(8,128)(2,1)} %bitcast.1, f32[256]{0:T(256)} %space_gain.1, f32[256]{0:T(256)} %space_bias.1, bf16[3,256,256]{2,1,0:T(8,128)(2,1)} %time_kernel.1, f32[256]{0:T(256)} %time_gain.1, f32[256]{0:T(256)} %time_bias.1), custom_call_target="tpu_custom_call" | custom-call | tf_op jit(solution)/shard_map/pallas_call | solution.py:341
  25.7 1.3 %copy.9 = bf16[2,16,128,256]{3,2,1,0:T(8,128)(2,1)} copy(bf16[2,16,128,256]{3,2,1,0:T(8,128)(2,1)S(1)} %shard_map.73) | data formatting | bytes 4194304

commit v6 on v5

--- a/solution.py
+++ b/solution.py
@@ -54,15 +54,17 @@
                 barrier, inc=1, device_id=device, device_id_type=pl.DeviceIdType.MESH
             )
 
-    def rows_start(first, count, sem, start=0, size=frames, step=None):
+    def rows_start(first, count, sem, start=0, size=frames, step=None, width=cols):
         step = step or count
         for f in range(start, start + size):
             for row in range(first, first + count, step):
-                pltpu.make_async_copy(
-                    features.at[f, pl.ds(row, step)],
-                    feat.at[pl.ds(row + 1, step), f],
-                    feat_sem.at[sem],
-                ).start()
+                for left in range(0, cols, width):
+                    columns = pl.ds(left, width)
+                    pltpu.make_async_copy(
+                        features.at[f, pl.ds(row, step), columns],
+                        feat.at[pl.ds(row + 1, step), f, columns],
+                        feat_sem.at[sem],
+                    ).start()
 
     def rows_wait(first, count, sem, start=0, size=frames):
         block = feat.at[pl.ds(first + 1, count), pl.ds(start, size)]
@@ -79,10 +81,10 @@
             wspace.at[pl.ds(start, count)],
             weight_sem.at[sem],
         )
-        for start, count, sem in ((0, 4, 1), (4, 5, 2))
+        for start, count, sem in ((0, 3, 1), (3, 6, 2))
     ]
     lags_copy = pltpu.make_async_copy(time_kernel, wtime, feat_sem.at[2])
-    rows_start(0, 3, 0, 0, split, 1)
+    rows_start(0, 3, 0, 0, split, 1, half)
     for copy in vector_copies:
         copy.start()
     greet(*neighbours[2])
@@ -220,13 +222,13 @@
 
     @once
     def _():
-        begun[...] = taps((1,), ((0, 0, 3), (1, 0, 1)), 0, split)
+        begun[...] = taps((1,), ((0, 0, 3),), 0, split)
 
     space_copies[1].wait()
 
     @once
     def _():
-        rest = taps((1,), ((1, 1, 3), (2, 0, 3)), 0, split)
+        rest = taps((1,), ((1, 0, 3), (2, 0, 3)), 0, split)
         space_store(1, begun[...] + rest, 0, split)
 
     peers = (

time: 27.2 us -> 27.2 us (level)
  no operation moved by 1% of the time
where the time goes in v6:
time: 27.2 us; the launch traced here: 27 us
  Pallas kernels  25.7 us (94%)
  local copies, waits for them, and re-layouts  1.32 us (5%)
    pallas_call x1, Pallas kernels, body(): pl.pallas_call(kernel, out_shape=jax.ShapeDtypeStruct(features.shape, bf1...  25.7 us
    unnamed x1, local copies, waits for them, and re-layouts  1.32 us

profile of v6, /device:TPU:1, one launch (start us, length us, event | category | flops | bytes accessed | tf_op | source)
XLA Modules:
  0.0 27.0 jit_solution(14388253078122680898)
XLA Ops:
  0.0 25.7 %shard_map.73 = bf16[2,16,128,256]{3,2,1,0:T(8,128)(2,1)S(1)} custom-call(bf16[2,16,128,256]{3,2,1,0:T(8,128)(2,1)} %features.1, bf16[9,256,256]{2,1,0:T(8,128)(2,1)} %bitcast.1, f32[256]{0:T(256)} %space_gain.1, f32[256]{0:T(256)} %space_bias.1, bf16[3,256,256]{2,1,0:T(8,128)(2,1)} %time_kernel.1, f32[256]{0:T(256)} %time_gain.1, f32[256]{0:T(256)} %time_bias.1), custom_call_target="tpu_custom_call" | custom-call | tf_op jit(solution)/shard_map/pallas_call | solution.py:343
  25.7 1.3 %copy.9 = bf16[2,16,128,256]{3,2,1,0:T(8,128)(2,1)} copy(bf16[2,16,128,256]{3,2,1,0:T(8,128)(2,1)S(1)} %shard_map.73) | data formatting | bytes 4194304

commit v7 on v6

--- a/solution.py
+++ b/solution.py
@@ -83,19 +83,20 @@
         )
         for start, count, sem in ((0, 3, 1), (3, 6, 2))
     ]
-    lags_copy = pltpu.make_async_copy(time_kernel, wtime, feat_sem.at[2])
+    lags_copy = pltpu.make_async_copy(time_kernel, wtime, feat_sem.at[1])
+    greet(*neighbours[2])
     rows_start(0, 3, 0, 0, split, 1, half)
     for copy in vector_copies:
         copy.start()
-    greet(*neighbours[2])
+    greet(*neighbours[3])
     for copy in space_copies:
         copy.start()
-    for i in (0, 1, 3):
+    for i in (0, 1):
         greet(*neighbours[i])
     rows_start(0, 4, 1, split, frames - split)
-    rows_start(3, 1, 2, 0, split)
-
-    time_send, up_send, down_send = (weight_sem.at[i] for i in range(3))
+    rows_start(3, 1, 1, 0, split)
+
+    time_send, halo_send = weight_sem.at[0], weight_sem.at[1]
     groups = group_starts(last)
 
     def time_copy(source, target, sem):
@@ -112,6 +113,11 @@
         source = ntime.at[row, pl.ds(frames - LAGS + start, count)]
         target = earlier.at[row, pl.ds(start, count)]
         pl.when(has_next)(time_copy(source, target, sem).start)
+
+    def halo_wait(sem):
+        for count, present in ((2, has_up & has_down), (1, has_up != has_down)):
+            block = feat.at[pl.ds(0, count)]
+            pl.when(present)(pltpu.make_async_copy(block, block, sem).wait)
 
     def time_wait(block, sem):
         pl.when(has_prev)(
@@ -241,19 +247,18 @@
 
     row_send(1, 0, 0, 1)
     to_up = pltpu.make_async_remote_copy(
-        features.at[:, 0], feat.at[rows + 1], up_send, halo_recv.at[0],
+        features.at[:, 0], feat.at[rows + 1], halo_send, halo_recv.at[0],
         device_id={"band": band - 1}, device_id_type=pl.DeviceIdType.MESH,
     )
     to_down = pltpu.make_async_remote_copy(
-        features.at[:, rows - 1], feat.at[0], down_send, halo_recv.at[1],
+        features.at[:, rows - 1], feat.at[0], halo_send, halo_recv.at[0],
         device_id={"band": band + 1}, device_id_type=pl.DeviceIdType.MESH,
     )
     pl.when(has_up)(to_up.start)
     pl.when(has_down)(to_down.start)
 
     rows_start(4, rows - 4, 0)
-    rows_wait(0, 4, 1, split, frames - split)
-    rows_wait(3, 1, 2, 0, split)
+    rows_wait(0, 4 * (frames - split) + split, 1, 0, 1)
     lags_copy.start()
 
     @once
@@ -278,8 +283,7 @@
         space_part((row,))
         row_send(row, sum((row >= g).astype(jnp.int32) for g in groups[1:]))
 
-    pl.when(has_up)(to_down.wait_recv)
-    pl.when(has_down)(to_up.wait_recv)
+    halo_wait(halo_recv.at[0])
 
     @once
     def _():
@@ -328,8 +332,7 @@
                 total += earlier[last, f, columns].astype(jnp.float32)
             finish(last, f, total, side * half, half)
 
-    pl.when(has_up)(to_up.wait_send)
-    pl.when(has_down)(to_down.wait_send)
+    halo_wait(halo_send)
 
     @pl.when(has_next)
     def _():
@@ -356,9 +359,9 @@
             pltpu.VMEM(rest[0].shape, bf16),
             pltpu.VMEM(rest[3].shape, bf16),
             pltpu.VMEM((4, channels), jnp.float32),
+            pltpu.SemaphoreType.DMA((2,)),
             pltpu.SemaphoreType.DMA((3,)),
-            pltpu.SemaphoreType.DMA((3,)),
-            pltpu.SemaphoreType.DMA((2,)),
+            pltpu.SemaphoreType.DMA((1,)),
             pltpu.SemaphoreType.DMA((len(group_starts(rows - 1)) + 2,)),
         ],
         compiler_params=pltpu.CompilerParams(

time: 27.2 us -> 27.2 us (level)
  no operation moved by 1% of the time
where the time goes in v7:
time: 27.2 us; the launch traced here: 27 us
  Pallas kernels  25.7 us (94%)
  local copies, waits for them, and re-layouts  1.32 us (5%)
    pallas_call x1, Pallas kernels, body(): pl.pallas_call(kernel, out_shape=jax.ShapeDtypeStruct(features.shape, bf1...  25.7 us
    unnamed x1, local copies, waits for them, and re-layouts  1.32 us

profile of v7, /device:TPU:1, one launch (start us, length us, event | category | flops | bytes accessed | tf_op | source)
XLA Modules:
  0.0 27.0 jit_solution(13077146134907781266)
XLA Ops:
  0.0 25.7 %shard_map.73 = bf16[2,16,128,256]{3,2,1,0:T(8,128)(2,1)S(1)} custom-call(bf16[2,16,128,256]{3,2,1,0:T(8,128)(2,1)} %features.1, bf16[9,256,256]{2,1,0:T(8,128)(2,1)} %bitcast.1, f32[256]{0:T(256)} %space_gain.1, f32[256]{0:T(256)} %space_bias.1, bf16[3,256,256]{2,1,0:T(8,128)(2,1)} %time_kernel.1, f32[256]{0:T(256)} %time_gain.1, f32[256]{0:T(256)} %time_bias.1), custom_call_target="tpu_custom_call" | custom-call | tf_op jit(solution)/shard_map/pallas_call | solution.py:346
  25.7 1.3 %copy.9 = bf16[2,16,128,256]{3,2,1,0:T(8,128)(2,1)} copy(bf16[2,16,128,256]{3,2,1,0:T(8,128)(2,1)S(1)} %shard_map.73) | data formatting | bytes 4194304

commit v8 on v7

--- a/solution.py
+++ b/solution.py
@@ -84,14 +84,13 @@
         for start, count, sem in ((0, 3, 1), (3, 6, 2))
     ]
     lags_copy = pltpu.make_async_copy(time_kernel, wtime, feat_sem.at[1])
-    greet(*neighbours[2])
     rows_start(0, 3, 0, 0, split, 1, half)
     for copy in vector_copies:
         copy.start()
-    greet(*neighbours[3])
+    greet(*neighbours[2])
     for copy in space_copies:
         copy.start()
-    for i in (0, 1):
+    for i in (0, 1, 3):
         greet(*neighbours[i])
     rows_start(0, 4, 1, split, frames - split)
     rows_start(3, 1, 1, 0, split)

time: 27.2 us -> 27.2 us (level)
  no operation moved by 1% of the time
where the time goes in v8:
time: 27.2 us; the launch traced here: 27 us
  Pallas kernels  25.7 us (94%)
  local copies, waits for them, and re-layouts  1.32 us (5%)
    pallas_call x1, Pallas kernels, body(): pl.pallas_call(kernel, out_shape=jax.ShapeDtypeStruct(features.shape, bf1...  25.7 us
    unnamed x1, local copies, waits for them, and re-layouts  1.32 us

profile of v8, /device:TPU:1, one launch (start us, length us, event | category | flops | bytes accessed | tf_op | source)
XLA Modules:
  0.0 27.0 jit_solution(15855359014106900840)
XLA Ops:
  0.0 25.7 %shard_map.73 = bf16[2,16,128,256]{3,2,1,0:T(8,128)(2,1)S(1)} custom-call(bf16[2,16,128,256]{3,2,1,0:T(8,128)(2,1)} %features.1, bf16[9,256,256]{2,1,0:T(8,128)(2,1)} %bitcast.1, f32[256]{0:T(256)} %space_gain.1, f32[256]{0:T(256)} %space_bias.1, bf16[3,256,256]{2,1,0:T(8,128)(2,1)} %time_kernel.1, f32[256]{0:T(256)} %time_gain.1, f32[256]{0:T(256)} %time_bias.1), custom_call_target="tpu_custom_call" | custom-call | tf_op jit(solution)/shard_map/pallas_call | solution.py:345
  25.7 1.3 %copy.9 = bf16[2,16,128,256]{3,2,1,0:T(8,128)(2,1)} copy(bf16[2,16,128,256]{3,2,1,0:T(8,128)(2,1)S(1)} %shard_map.73) | data formatting | bytes 4194304

commit v9 on v6

--- a/solution.py
+++ b/solution.py
@@ -54,7 +54,9 @@
                 barrier, inc=1, device_id=device, device_id_type=pl.DeviceIdType.MESH
             )
 
-    def rows_start(first, count, sem, start=0, size=frames, step=None, width=cols):
+    def rows_start(
+        first, count, sem, start=0, size=frames, step=None, width=cols, priority=0
+    ):
         step = step or count
         for f in range(start, start + size):
             for row in range(first, first + count, step):
@@ -64,7 +66,7 @@
                         features.at[f, pl.ds(row, step), columns],
                         feat.at[pl.ds(row + 1, step), f, columns],
                         feat_sem.at[sem],
-                    ).start()
+                    ).start(priority=priority)
 
     def rows_wait(first, count, sem, start=0, size=frames):
         block = feat.at[pl.ds(first + 1, count), pl.ds(start, size)]
@@ -88,12 +90,12 @@
     for copy in vector_copies:
         copy.start()
     greet(*neighbours[2])
-    for copy in space_copies:
-        copy.start()
+    for i, copy in enumerate(space_copies):
+        copy.start(priority=i)
     for i in (0, 1, 3):
         greet(*neighbours[i])
-    rows_start(0, 4, 1, split, frames - split)
-    rows_start(3, 1, 2, 0, split)
+    rows_start(0, 4, 1, split, frames - split, priority=1)
+    rows_start(3, 1, 2, 0, split, priority=1)
 
     time_send, up_send, down_send = (weight_sem.at[i] for i in range(3))
     groups = group_starts(last)

time: 27.2 us -> 27.2 us (level)
  no operation moved by 1% of the time
where the time goes in v9:
time: 27.2 us; the launch traced here: 27 us
  Pallas kernels  25.7 us (94%)
  local copies, waits for them, and re-layouts  1.32 us (5%)
    pallas_call x1, Pallas kernels, body(): pl.pallas_call(kernel, out_shape=jax.ShapeDtypeStruct(features.shape, bf1...  25.7 us
    unnamed x1, local copies, waits for them, and re-layouts  1.32 us

profile of v9, /device:TPU:1, one launch (start us, length us, event | category | flops | bytes accessed | tf_op | source)
XLA Modules:
  0.0 27.0 jit_solution(13725480554916174855)
XLA Ops:
  0.0 25.7 %shard_map.73 = bf16[2,16,128,256]{3,2,1,0:T(8,128)(2,1)S(1)} custom-call(bf16[2,16,128,256]{3,2,1,0:T(8,128)(2,1)} %features.1, bf16[9,256,256]{2,1,0:T(8,128)(2,1)} %bitcast.1, f32[256]{0:T(256)} %space_gain.1, f32[256]{0:T(256)} %space_bias.1, bf16[3,256,256]{2,1,0:T(8,128)(2,1)} %time_kernel.1, f32[256]{0:T(256)} %time_gain.1, f32[256]{0:T(256)} %time_bias.1), custom_call_target="tpu_custom_call" | custom-call | tf_op jit(solution)/shard_map/pallas_call | solution.py:345
  25.7 1.3 %copy.9 = bf16[2,16,128,256]{3,2,1,0:T(8,128)(2,1)} copy(bf16[2,16,128,256]{3,2,1,0:T(8,128)(2,1)S(1)} %shard_map.73) | data formatting | bytes 4194304

commit v10 on v8

--- a/solution.py
+++ b/solution.py
@@ -54,7 +54,9 @@
                 barrier, inc=1, device_id=device, device_id_type=pl.DeviceIdType.MESH
             )
 
-    def rows_start(first, count, sem, start=0, size=frames, step=None, width=cols):
+    def rows_start(
+        first, count, sem, start=0, size=frames, step=None, width=cols, priority=0
+    ):
         step = step or count
         for f in range(start, start + size):
             for row in range(first, first + count, step):
@@ -64,7 +66,7 @@
                         features.at[f, pl.ds(row, step), columns],
                         feat.at[pl.ds(row + 1, step), f, columns],
                         feat_sem.at[sem],
-                    ).start()
+                    ).start(priority=priority)
 
     def rows_wait(first, count, sem, start=0, size=frames):
         block = feat.at[pl.ds(first + 1, count), pl.ds(start, size)]
@@ -88,12 +90,12 @@
     for copy in vector_copies:
         copy.start()
     greet(*neighbours[2])
-    for copy in space_copies:
-        copy.start()
+    for i, copy in enumerate(space_copies):
+        copy.start(priority=i)
     for i in (0, 1, 3):
         greet(*neighbours[i])
-    rows_start(0, 4, 1, split, frames - split)
-    rows_start(3, 1, 1, 0, split)
+    rows_start(0, 4, 1, split, frames - split, priority=1)
+    rows_start(3, 1, 1, 0, split, priority=1)
 
     time_send, halo_send = weight_sem.at[0], weight_sem.at[1]
     groups = group_starts(last)

time: 27.2 us -> 27.2 us (level)
  no operation moved by 1% of the time
where the time goes in v10:
time: 27.2 us; the launch traced here: 27 us
  Pallas kernels  25.7 us (94%)
  local copies, waits for them, and re-layouts  1.32 us (5%)
    pallas_call x1, Pallas kernels, body(): pl.pallas_call(kernel, out_shape=jax.ShapeDtypeStruct(features.shape, bf1...  25.7 us
    unnamed x1, local copies, waits for them, and re-layouts  1.32 us

profile of v10, /device:TPU:1, one launch (start us, length us, event | category | flops | bytes accessed | tf_op | source)
XLA Modules:
  0.0 27.0 jit_solution(18337452811254049070)
XLA Ops:
  0.0 25.7 %shard_map.73 = bf16[2,16,128,256]{3,2,1,0:T(8,128)(2,1)S(1)} custom-call(bf16[2,16,128,256]{3,2,1,0:T(8,128)(2,1)} %features.1, bf16[9,256,256]{2,1,0:T(8,128)(2,1)} %bitcast.1, f32[256]{0:T(256)} %space_gain.1, f32[256]{0:T(256)} %space_bias.1, bf16[3,256,256]{2,1,0:T(8,128)(2,1)} %time_kernel.1, f32[256]{0:T(256)} %time_gain.1, f32[256]{0:T(256)} %time_bias.1), custom_call_target="tpu_custom_call" | custom-call | tf_op jit(solution)/shard_map/pallas_call | solution.py:347
  25.7 1.3 %copy.9 = bf16[2,16,128,256]{3,2,1,0:T(8,128)(2,1)} copy(bf16[2,16,128,256]{3,2,1,0:T(8,128)(2,1)S(1)} %shard_map.73) | data formatting | bytes 4194304

commit v11 on v6

--- a/solution.py
+++ b/solution.py
@@ -32,6 +32,7 @@
 ):
     frames, rows, cols, channels = features.shape
     half = cols // 2
+    pieces = ((0, cols - cols // 4), (cols - cols // 4, cols // 4))
     split = frames - LAGS + 1
     last = rows - 1
     band, bands = lax.axis_index("band"), lax.axis_size("band")
@@ -298,8 +299,8 @@
     @pl.when(has_next)
     def _():
         lag_sums(last)
-        for side in range(2):
-            columns = pl.ds(side * half, half)
+        for side, (left, width) in enumerate(pieces):
+            columns = pl.ds(left, width)
             time_copy(
                 partial.at[:, columns],
                 earlier.at[last, :, columns],
@@ -319,14 +320,14 @@
 
     time_part(0)
     totals = own_totals(last)
-    for side in range(2):
-        columns = slice(side * half, (side + 1) * half)
-        time_wait(earlier.at[last, :, pl.ds(side * half, half)], len(groups) + side)
+    for side, (left, width) in enumerate(pieces):
+        columns = slice(left, left + width)
+        time_wait(earlier.at[last, :, pl.ds(left, width)], len(groups) + side)
         for f in range(frames):
             total = totals[f][columns]
             if f < LAGS:
                 total += earlier[last, f, columns].astype(jnp.float32)
-            finish(last, f, total, side * half, half)
+            finish(last, f, total, left, width)
 
     pl.when(has_up)(to_up.wait_send)
     pl.when(has_down)(to_down.wait_send)

time: 27.2 us -> 27.2 us (level)
  no operation moved by 1% of the time
where the time goes in v11:
time: 27.2 us; the launch traced here: 27 us
  Pallas kernels  25.7 us (94%)
  local copies, waits for them, and re-layouts  1.32 us (5%)
    pallas_call x1, Pallas kernels, body(): pl.pallas_call(kernel, out_shape=jax.ShapeDtypeStruct(features.shape, bf1...  25.7 us
    unnamed x1, local copies, waits for them, and re-layouts  1.32 us

profile of v11, /device:TPU:1, one launch (start us, length us, event | category | flops | bytes accessed | tf_op | source)
XLA Modules:
  0.0 27.0 jit_solution(12133030795766340288)
XLA Ops:
  0.0 25.7 %shard_map.73 = bf16[2,16,128,256]{3,2,1,0:T(8,128)(2,1)S(1)} custom-call(bf16[2,16,128,256]{3,2,1,0:T(8,128)(2,1)} %features.1, bf16[9,256,256]{2,1,0:T(8,128)(2,1)} %bitcast.1, f32[256]{0:T(256)} %space_gain.1, f32[256]{0:T(256)} %space_bias.1, bf16[3,256,256]{2,1,0:T(8,128)(2,1)} %time_kernel.1, f32[256]{0:T(256)} %time_gain.1, f32[256]{0:T(256)} %time_bias.1), custom_call_target="tpu_custom_call" | custom-call | tf_op jit(solution)/shard_map/pallas_call | solution.py:344
  25.7 1.3 %copy.9 = bf16[2,16,128,256]{3,2,1,0:T(8,128)(2,1)} copy(bf16[2,16,128,256]{3,2,1,0:T(8,128)(2,1)S(1)} %shard_map.73) | data formatting | bytes 4194304

commit v12 on v10

--- a/solution.py
+++ b/solution.py
@@ -32,6 +32,7 @@
 ):
     frames, rows, cols, channels = features.shape
     half = cols // 2
+    pieces = ((0, cols - cols // 4), (cols - cols // 4, cols // 4))
     split = frames - LAGS + 1
     last = rows - 1
     band, bands = lax.axis_index("band"), lax.axis_size("band")
@@ -303,8 +304,8 @@
     @pl.when(has_next)
     def _():
         lag_sums(last)
-        for side in range(2):
-            columns = pl.ds(side * half, half)
+        for side, (left, width) in enumerate(pieces):
+            columns = pl.ds(left, width)
             time_copy(
                 partial.at[:, columns],
                 earlier.at[last, :, columns],
@@ -324,14 +325,14 @@
 
     time_part(0)
     totals = own_totals(last)
-    for side in range(2):
-        columns = slice(side * half, (side + 1) * half)
-        time_wait(earlier.at[last, :, pl.ds(side * half, half)], len(groups) + side)
+    for side, (left, width) in enumerate(pieces):
+        columns = slice(left, left + width)
+        time_wait(earlier.at[last, :, pl.ds(left, width)], len(groups) + side)
         for f in range(frames):
             total = totals[f][columns]
             if f < LAGS:
                 total += earlier[last, f, columns].astype(jnp.float32)
-            finish(last, f, total, side * half, half)
+            finish(last, f, total, left, width)
 
     halo_wait(halo_send)
 

time: 27.2 us -> 27.2 us (level)
  no operation moved by 1% of the time
where the time goes in v12:
time: 27.2 us; the launch traced here: 27 us
  Pallas kernels  25.7 us (94%)
  local copies, waits for them, and re-layouts  1.32 us (5%)
    pallas_call x1, Pallas kernels, body(): pl.pallas_call(kernel, out_shape=jax.ShapeDtypeStruct(features.shape, bf1...  25.7 us
    unnamed x1, local copies, waits for them, and re-layouts  1.32 us

profile of v12, /device:TPU:1, one launch (start us, length us, event | category | flops | bytes accessed | tf_op | source)
XLA Modules:
  0.0 27.0 jit_solution(16480349432978739386)
XLA Ops:
  0.0 25.7 %shard_map.73 = bf16[2,16,128,256]{3,2,1,0:T(8,128)(2,1)S(1)} custom-call(bf16[2,16,128,256]{3,2,1,0:T(8,128)(2,1)} %features.1, bf16[9,256,256]{2,1,0:T(8,128)(2,1)} %bitcast.1, f32[256]{0:T(256)} %space_gain.1, f32[256]{0:T(256)} %space_bias.1, bf16[3,256,256]{2,1,0:T(8,128)(2,1)} %time_kernel.1, f32[256]{0:T(256)} %time_gain.1, f32[256]{0:T(256)} %time_bias.1), custom_call_target="tpu_custom_call" | custom-call | tf_op jit(solution)/shard_map/pallas_call | solution.py:348
  25.7 1.3 %copy.9 = bf16[2,16,128,256]{3,2,1,0:T(8,128)(2,1)} copy(bf16[2,16,128,256]{3,2,1,0:T(8,128)(2,1)S(1)} %shard_map.73) | data formatting | bytes 4194304
